TPU v7x, 512 devices: a whole 4x4x16 slice. The times are simulated.
512 devices in a mesh: row: 32 (over z, core), col: 16 (over x, y).
Axes of the slice: x: 4, y: 4, z: 16, core: 2. Of those that a mesh axis runs over, the one named last changes fastest.
Arguments:
- x_points: bfloat16 [131072, 256], P(('row', 'col')), may hold values from -1.5 to 1.5
- y_points: bfloat16 [131072, 256], P(('row', 'col')), may hold values from -1.5 to 1.5
- log_a: float32 [131072], P(('row', 'col')), may hold values from -1.5 to 1.5
- log_b: float32 [131072], P(('row', 'col')), may hold values from -1.5 to 1.5
- g_init: float32 [131072], P(('row', 'col')), may hold values from -3 to 3
- tile_list: int32 [24576, 2], P(('row', 'col')), may hold values from 0 to 1023, as said below
- tile_count: int32 [512], P(('row', 'col')), may hold values from 2 to 48, as said below
Outputs:
- f_out: float32 [131072], P(('row', 'col'))
- g_out: float32 [131072], P(('row', 'col'))
Inputs may be any that keep to these rules, and one draw needn't show every extreme that they name: `tile_list`: slots 48 * d to 48 * (d + 1) - 1 belong to device d = row index * 16 + col index. Each slot names a source block held by a device of d's row group and a target block held by a device of d's col group; the slots of one device are distinct pairs. Every block of either cloud is in some active tile. `tile_count`: some device has all 48 slots active.
All inputs are finite; a program needn't handle non-finite values.
Results may differ from a plain program's by a relative error of at most 0.0003.
Values may be sent and summed in bfloat16 or wider, within the bound.
A program may use at most 64 MiB of HBM per device.

v0:
```python
import math
import jax
import jax.numpy as jnp
from jax import lax
from jax.sharding import PartitionSpec as P

BLOCK = 128
ITERS = 2
EPSILON = 0.25
NEGATIVE = -1e30


def block_costs(x_blocks, x_square, y_blocks, y_square, rows, cols):
    x_take = jnp.take(x_blocks, rows, axis=0)
    y_take = jnp.take(y_blocks, cols, axis=0)
    inner = jnp.einsum("tpd,tqd->tpq", x_take, y_take, preferred_element_type=jnp.float32)
    return (
        0.5 * jnp.take(x_square, rows, axis=0)[:, :, None]
        + 0.5 * jnp.take(y_square, cols, axis=0)[:, None, :]
        - inner
    )


def local_max(score_of, targets, shape_blocks, turns):

    def visit(turn_index, acc):
        return acc.at[targets[turn_index]].max(jnp.max(score_of(turn_index), axis=-1))

    return lax.fori_loop(0, turns, visit, jnp.full(shape_blocks, NEGATIVE, jnp.float32))


def local_sum(score_of, targets, top, turns):

    def visit(turn_index, acc):
        rows = targets[turn_index]
        shift = jnp.take(top, rows, axis=0)[:, :, None]
        return acc.at[rows].add(jnp.sum(jnp.exp(score_of(turn_index) - shift), axis=-1))

    return lax.fori_loop(0, turns, visit, jnp.zeros(top.shape, jnp.float32))


def row_potential(score_of, targets, shape_blocks, turns):
    top = lax.pmax(local_max(score_of, targets, shape_blocks, turns), "col")
    total = lax.psum(local_sum(score_of, targets, top, turns), "col")
    return -EPSILON * (top + jnp.log(total))


def col_potential(score_of, targets, shape_blocks, turns):
    top = lax.pmax(
        local_max(score_of, targets, shape_blocks, turns).astype(jnp.bfloat16), "row"
    ).astype(jnp.float32)
    total = lax.psum(local_sum(score_of, targets, top, turns), "row")
    return -EPSILON * (top + jnp.log(total))


def body(x_points, y_points, log_a, log_b, g_init, tile_list, tile_count):
    width = x_points.shape[1]
    points_here = x_points.shape[0]
    per_device = points_here // BLOCK
    row_index = lax.axis_index("row")
    col_index = lax.axis_index("col")
    col_count = lax.axis_size("col")
    x_all = lax.all_gather(x_points, "col", axis=0, tiled=True)
    a_all = lax.all_gather(log_a, "col", axis=0, tiled=True)
    y_all = lax.all_gather(y_points, "row", axis=0, tiled=True)
    y_extra = lax.all_gather(jnp.stack([log_b, g_init]), "row", axis=1, tiled=True)
    x_blocks = x_all.reshape(-1, BLOCK, width)
    y_blocks = y_all.reshape(-1, BLOCK, width)
    x_square = jnp.einsum("bpd,bpd->bp", x_blocks, x_blocks, preferred_element_type=jnp.float32)
    y_square = jnp.einsum("bpd,bpd->bp", y_blocks, y_blocks, preferred_element_type=jnp.float32)
    a_blocks = a_all.reshape(-1, BLOCK)
    b_blocks = y_extra[0].reshape(-1, BLOCK)
    g_blocks = y_extra[1].reshape(-1, BLOCK)
    tiles_here = tile_list.shape[0]
    batch = math.gcd(tiles_here, 8)
    turns = tiles_here // batch
    row_ids = (tile_list[:, 0] - row_index * (col_count * per_device)).reshape(turns, batch)
    col_global = tile_list[:, 1]
    col_ids = (
        col_global // per_device // col_count * per_device + col_global % per_device
    ).reshape(turns, batch)
    active = (jnp.arange(tiles_here, dtype=jnp.int32) < tile_count[0]).reshape(turns, batch)

    def costs_at(turn_index):
        return block_costs(
            x_blocks, x_square, y_blocks, y_square, row_ids[turn_index], col_ids[turn_index]
        )

    f_blocks = jnp.zeros_like(a_blocks)
    for iteration in range(ITERS):

        def f_scores(turn_index):
            cols = col_ids[turn_index]
            scores = (
                jnp.take(g_blocks, cols, axis=0)[:, None, :] - costs_at(turn_index)
            ) / EPSILON + jnp.take(b_blocks, cols, axis=0)[:, None, :]
            return jnp.where(active[turn_index][:, None, None], scores, NEGATIVE)

        f_blocks = row_potential(f_scores, row_ids, a_blocks.shape, turns)

        def g_scores(turn_index):
            rows = row_ids[turn_index]
            scores = (
                jnp.take(f_blocks, rows, axis=0)[:, :, None] - costs_at(turn_index)
            ) / EPSILON + jnp.take(a_blocks, rows, axis=0)[:, :, None]
            scores = jnp.transpose(scores, (0, 2, 1))
            return jnp.where(active[turn_index][:, None, None], scores, NEGATIVE)

        g_blocks = col_potential(g_scores, col_ids, b_blocks.shape, turns)
    f_out = lax.dynamic_slice_in_dim(f_blocks.reshape(-1), col_index * points_here, points_here)
    g_out = lax.dynamic_slice_in_dim(g_blocks.reshape(-1), row_index * points_here, points_here)
    return (f_out, g_out)


def solution(mesh):
    in_specs = (
        P(("row", "col"), None),
        P(("row", "col"), None),
        P(("row", "col")),
        P(("row", "col")),
        P(("row", "col")),
        P(("row", "col"), None),
        P(("row", "col")),
    )
    out_specs = (P(("row", "col")), P(("row", "col")))
    return jax.shard_map(body, mesh=mesh, in_specs=in_specs, out_specs=out_specs, check_vma=False)
```

profile of v0, /device:TPU:1, one launch (start us, length us, event | category | flops | bytes accessed | tf_op | source)
XLA Modules:
  0.0 1156.1 jit_solution(3154675278406226549)
XLA Ops:
  10.2 19.6 %all-gather = f32[16,1,256]{2,1,0:T(1,128)S(1)} all-gather(f32[1,1,256]{2,1,0:T(1,128)} %bitcast.181), channel_id=1, replica_groups=mesh['row'=32,'col'=16] {'col'}, dimensions={0}, use_global_device_ids=true | all-gather | bytes 17408 | tf_op jit(solution)/shard_map/all_gather | solution.py:64
  30.5 41.8 %all_gather.12 = f32[2,8192]{1,0:T(2,128)S(1)} all-gather(f32[2,256]{1,0:T(2,128)S(1)} %pad_maximum_fusion), channel_id=1, replica_groups=mesh['row'=32,'col'=16] {'row'}, dimensions={1}, use_global_device_ids=true | all-gather | bytes 67584 | tf_op jit(solution)/shard_map/all_gather | solution.py:66
  77.3 74.6 %all-gather.6.cloned.1.call-done = bf16[8192,256]{1,0:T(8,128)(2,1)} async-done(((bf16[256,256]{1,0:T(8,128)(2,1)}), bf16[8192,256]{1,0:T(8,128)(2,1)}) %all-gather.6.cloned.1.call-update) | async-done | bytes 4194320 | tf_op jit(solution)/shard_map/all_gather | solution.py:65
  151.9 3.3 fusion.112
  155.2 42.2 %while.104 = (s32[]{:T(128)}, f32[32,128]{1,0:T(8,128)S(1)}, s32[6,8]{1,0:T(8,128)S(1)}, pred[6,8]{1,0:T(8,128)(4,1)S(1)}, s32[6,8]{1,0:T(8,128)S(1)}, /*index=5...) while((s32[]{:T(128)}, f32[32,128]{1,0:T(8,128)S(1)}, ...), condition=%wide.region_3.8_spmd, body=%wide.region_0.7_spmd.sunk | while | flops 68558968 | bytes 3252905 | solution.py:29
  197.5 60.4 %pmax.28 = f32[32,128]{1,0:T(8,128)S(1)} all-reduce(f32[32,128]{1,0:T(8,128)S(1)} %get-tuple-element.1538), channel_id=1, replica_groups=mesh['row'=32,'col'=16] {'col'}, use_global_device_ids=true, to_apply=%region_4.9 | all-reduce | flops 4096 | bytes 32768 | tf_op jit(solution)/shard_map/pmax | solution.py:43
  257.9 45.7 %while.105 = (s32[]{:T(128)}, f32[32,128]{1,0:T(8,128)S(1)}, s32[6,8]{1,0:T(8,128)S(1)}, pred[6,8]{1,0:T(8,128)(4,1)S(1)}, s32[6,8]{1,0:T(8,128)S(1)}, /*index=5...) while((s32[]{:T(128)}, f32[32,128]{1,0:T(8,128)S(1)}, ...), condition=%wide.region_8.13_spmd, body=%wide.region_5.12_spmd.sunk | while | flops 68691064 | bytes 3273425 | solution.py:39
  303.6 56.0 %psum.28 = f32[32,128]{1,0:T(8,128)S(1)} all-reduce(f32[32,128]{1,0:T(8,128)S(1)} %get-tuple-element.1539), channel_id=1, replica_groups=mesh['row'=32,'col'=16] {'col'}, use_global_device_ids=true, to_apply=%region_9.14 | all-reduce | flops 4096 | bytes 32768 | tf_op jit(solution)/shard_map/psum | solution.py:44
  359.6 42.5 %while.106 = (s32[]{:T(128)}, f32[64,128]{1,0:T(8,128)S(1)}, s32[6,8]{1,0:T(8,128)S(1)}, pred[6,8]{1,0:T(8,128)(4,1)S(1)}, s32[6,8]{1,0:T(8,128)S(1)}, /*index=5...) while((s32[]{:T(128)}, f32[64,128]{1,0:T(8,128)S(1)}, ...), condition=%wide.region_13.18_spmd, body=%wide.region_10.17_spmd.sunk | while | flops 68558968 | bytes 3252905 | solution.py:29
  362.6 2.8 gather_fusion.14
  369.7 2.8 gather_fusion.14
  391.0 2.8 gather_fusion.14
  398.1 2.8 gather_fusion.14
  402.2 114.2 %pmax.29 = bf16[64,128]{1,0:T(8,128)(2,1)S(1)} all-reduce(bf16[64,128]{1,0:T(8,128)(2,1)S(1)} %convert_element_type.12), channel_id=1, replica_groups=mesh['row'=32,'col'=16] {'row'}, use_global_device_ids=true, to_apply=%region_14.19 | all-reduce | flops 8192 | bytes 32768 | tf_op jit(solution)/shard_map/pmax | solution.py:49
  516.4 45.9 %while.107 = (s32[]{:T(128)}, f32[64,128]{1,0:T(8,128)S(1)}, s32[6,8]{1,0:T(8,128)S(1)}, pred[6,8]{1,0:T(8,128)(4,1)S(1)}, s32[6,8]{1,0:T(8,128)S(1)}, /*index=5...) while((s32[]{:T(128)}, f32[64,128]{1,0:T(8,128)S(1)}, ...), condition=%wide.region_18.23_spmd, body=%wide.region_15.22_spmd.sunk | while | flops 68691064 | bytes 3273425 | solution.py:39
  562.3 90.0 %psum.29 = f32[64,128]{1,0:T(8,128)S(1)} all-reduce(f32[64,128]{1,0:T(8,128)S(1)} %get-tuple-element.1541), channel_id=1, replica_groups=mesh['row'=32,'col'=16] {'row'}, use_global_device_ids=true, to_apply=%region_19.24 | all-reduce | flops 8192 | bytes 65536 | tf_op jit(solution)/shard_map/psum | solution.py:52
  652.3 42.2 %while.108 = (s32[]{:T(128)}, f32[32,128]{1,0:T(8,128)S(1)}, s32[6,8]{1,0:T(8,128)S(1)}, pred[6,8]{1,0:T(8,128)(4,1)S(1)}, s32[6,8]{1,0:T(8,128)S(1)}, /*index=5...) while((s32[]{:T(128)}, f32[32,128]{1,0:T(8,128)S(1)}, ...), condition=%wide.region_23.28_spmd, body=%wide.region_20.27_spmd.sunk | while | flops 68558968 | bytes 3252905 | solution.py:29
  694.6 55.7 %pmax.30 = f32[32,128]{1,0:T(8,128)S(1)} all-reduce(f32[32,128]{1,0:T(8,128)S(1)} %get-tuple-element.1542), channel_id=1, replica_groups=mesh['row'=32,'col'=16] {'col'}, use_global_device_ids=true, to_apply=%region_24.29 | all-reduce | flops 4096 | bytes 32768 | tf_op jit(solution)/shard_map/pmax | solution.py:43
  750.3 45.7 %while.109 = (s32[]{:T(128)}, f32[32,128]{1,0:T(8,128)S(1)}, s32[6,8]{1,0:T(8,128)S(1)}, pred[6,8]{1,0:T(8,128)(4,1)S(1)}, s32[6,8]{1,0:T(8,128)S(1)}, /*index=5...) while((s32[]{:T(128)}, f32[32,128]{1,0:T(8,128)S(1)}, ...), condition=%wide.region_28.33_spmd, body=%wide.region_25.32_spmd.sunk | while | flops 68691064 | bytes 3273425 | solution.py:39
  795.9 56.0 %psum.30 = f32[32,128]{1,0:T(8,128)S(1)} all-reduce(f32[32,128]{1,0:T(8,128)S(1)} %get-tuple-element.1543), channel_id=1, replica_groups=mesh['row'=32,'col'=16] {'col'}, use_global_device_ids=true, to_apply=%region_29.34 | all-reduce | flops 4096 | bytes 32768 | tf_op jit(solution)/shard_map/psum | solution.py:44
  851.9 42.5 %while.110 = (s32[]{:T(128)}, f32[64,128]{1,0:T(8,128)S(1)}, s32[6,8]{1,0:T(8,128)S(1)}, pred[6,8]{1,0:T(8,128)(4,1)S(1)}, s32[6,8]{1,0:T(8,128)S(1)}, /*index=5...) while((s32[]{:T(128)}, f32[64,128]{1,0:T(8,128)S(1)}, ...), condition=%wide.region_33.38_spmd, body=%wide.region_30.37_spmd.sunk | while | flops 68558968 | bytes 3252905 | solution.py:29
  894.5 117.5 %pmax.31 = bf16[64,128]{1,0:T(8,128)(2,1)S(1)} all-reduce(bf16[64,128]{1,0:T(8,128)(2,1)S(1)} %convert_element_type.14), channel_id=1, replica_groups=mesh['row'=32,'col'=16] {'row'}, use_global_device_ids=true, to_apply=%region_34.39 | all-reduce | flops 8192 | bytes 32768 | tf_op jit(solution)/shard_map/pmax | solution.py:49
  1012.0 45.9 %while.111 = (s32[]{:T(128)}, f32[64,128]{1,0:T(8,128)S(1)}, s32[6,8]{1,0:T(8,128)S(1)}, pred[6,8]{1,0:T(8,128)(4,1)S(1)}, s32[6,8]{1,0:T(8,128)S(1)}, /*index=5...) while((s32[]{:T(128)}, f32[64,128]{1,0:T(8,128)S(1)}, ...), condition=%wide.region_38.43_spmd, body=%wide.region_35.42_spmd.sunk | while | flops 68691064 | bytes 3273425 | solution.py:39
  1057.9 90.0 %psum.31 = f32[64,128]{1,0:T(8,128)S(1)} all-reduce(f32[64,128]{1,0:T(8,128)S(1)} %get-tuple-element.1545), channel_id=1, replica_groups=mesh['row'=32,'col'=16] {'row'}, use_global_device_ids=true, to_apply=%region_39.44 | all-reduce | flops 8192 | bytes 65536 | tf_op jit(solution)/shard_map/psum | solution.py:52
  (773 shorter events, 347.0 us)
Async XLA Ops:
  7.2 67.8 %all-gather.4.cloned.1.call-start = ((), (), s32[]{:S(2)}) async-start(), calls=%async_computation | async-start | bytes 2228224 | tf_op jit(solution)/shard_map/all_gather | solution.py:63
  7.9 144.0 %all-gather.6.cloned.1.call-start = ((), (), s32[]{:S(2)}) async-start(), calls=%async_computation.1 | async-start | bytes 4325376 | tf_op jit(solution)/shard_map/all_gather | solution.py:65
  75.0 80.3 %copy-start = (bf16[4096,256]{1,0:T(8,128)(2,1)S(1)}, bf16[4096,256]{1,0:T(8,128)(2,1)}, u32[]{:S(2)}) copy-start(bf16[4096,256]{1,0:T(8,128)(2,1)} %all-gather.4.cloned.1.call-done) | copy-start | bytes 6291460
Sparse Core Ops, SparseCore 0:
  11.0 63.9 all-gather.3
  77.1 74.7 all-gather.5
where the time goes:
time: 1160 us
  blocking collectives  701 us (60%)
  local copies, waits for them, and re-layouts  283 us (24%)
  waiting for transfers between devices  78.4 us (7%)
  other arithmetic  47.9 us (4%)
  matrix products  26.8 us (2%)
  between operations  14.9 us (1%)
    pmax x2, blocking collectives, col_potential(): lax.pmax(local_max(score_of, targets, shape_blocks, turns).astype(jnp.bfl...  232 us
    psum x2, blocking collectives, col_potential(): total = lax.psum(local_sum(score_of, targets, top, turns), 'row')  180 us
    gather x48, local copies, waits for them, and re-layouts, block_costs(): y_take = jnp.take(y_blocks, cols, axis=0)  133 us
    pmax x2, blocking collectives, row_potential(): top = lax.pmax(local_max(score_of, targets, shape_blocks, turns), 'col')  116 us
    psum x2, blocking collectives, row_potential(): total = lax.psum(local_sum(score_of, targets, top, turns), 'col')  112 us
    all_gather x1, waiting for transfers between devices, body(): y_all = lax.all_gather(y_points, 'row', axis=0, tiled=True)  74.6 us
    all_gather x1, blocking collectives, body(): lax.all_gather(jnp.stack([log_b, g_init]), 'row', axis=1, tiled=True)  41.8 us
    gather x48, local copies, waits for them, and re-layouts, block_costs(): x_take = jnp.take(x_blocks, rows, axis=0)  27.8 us
  transfers between devices with their start and end apart: 2, of which 2 were waited for; matrix products, arithmetic and copies ran while one was open for 0% of the time, Pallas kernels for 0%

commit v1 on v0

--- a/solution.py
+++ b/solution.py
@@ -41,7 +41,7 @@
 
 def row_potential(score_of, targets, shape_blocks, turns):
     top = lax.pmax(local_max(score_of, targets, shape_blocks, turns), "col")
-    total = lax.psum(local_sum(score_of, targets, top, turns), "col")
+    total = jnp.sum(lax.all_gather(local_sum(score_of, targets, top, turns), "col"), axis=0)
     return -EPSILON * (top + jnp.log(total))
 
 

time: 1160 us -> 1070 us (0.922)
  blocking collectives: 701 us -> 606 us
    psum x2 -> x0, blocking collectives: 112 us -> none  [row_potential(): total = lax.psum(local_sum(score_of, targets, top, turns), 'col')]
    all_gather x0 -> x2, blocking collectives: none -> 31 us  [row_potential(): lax.all_gather(local_sum(score_of, targets, top, turns), 'col')]
    pmax x2, blocking collectives: 232 us -> 215 us  [col_potential(): lax.pmax(local_max(score_of, targets, shape_blocks, turns).astype(jnp.bfl...]
where the time goes in v1:
time: 1070 us; the launch traced here: 1060 us
  blocking collectives  606 us (57%)
  local copies, waits for them, and re-layouts  283 us (26%)
  waiting for transfers between devices  78.4 us (7%)
  other arithmetic  48 us (4%)
  matrix products  26.8 us (3%)
  between operations  14.9 us (1%)
    pmax x2, blocking collectives, col_potential(): lax.pmax(local_max(score_of, targets, shape_blocks, turns).astype(jnp.bfl...  215 us
    psum x2, blocking collectives, col_potential(): total = lax.psum(local_sum(score_of, targets, top, turns), 'row')  180 us
    gather x48, local copies, waits for them, and re-layouts, block_costs(): y_take = jnp.take(y_blocks, cols, axis=0)  133 us
    pmax x2, blocking collectives, row_potential(): top = lax.pmax(local_max(score_of, targets, shape_blocks, turns), 'col')  119 us
    all_gather x1, waiting for transfers between devices, body(): y_all = lax.all_gather(y_points, 'row', axis=0, tiled=True)  74.6 us
    all_gather x1, blocking collectives, body(): lax.all_gather(jnp.stack([log_b, g_init]), 'row', axis=1, tiled=True)  41.8 us
    all_gather x2, blocking collectives, row_potential(): lax.all_gather(local_sum(score_of, targets, top, turns), 'col')  31 us
    gather x48, local copies, waits for them, and re-layouts, block_costs(): x_take = jnp.take(x_blocks, rows, axis=0)  27.8 us
  transfers between devices with their start and end apart: 2, of which 2 were waited for; matrix products, arithmetic and copies ran while one was open for 0% of the time, Pallas kernels for 0%

profile of v1, /device:TPU:1, one launch (start us, length us, event | category | flops | bytes accessed | tf_op | source)
XLA Modules:
  0.0 1061.1 jit_solution(5173893655891534176)
XLA Ops:
  10.2 19.6 %all-gather.2 = f32[16,1,256]{2,1,0:T(1,128)S(1)} all-gather(f32[1,1,256]{2,1,0:T(1,128)} %bitcast.185), channel_id=1, replica_groups=mesh['row'=32,'col'=16] {'col'}, dimensions={0}, use_global_device_ids=true | all-gather | bytes 17408 | tf_op jit(solution)/shard_map/all_gather | solution.py:64
  30.5 41.8 %all_gather.24 = f32[2,8192]{1,0:T(2,128)S(1)} all-gather(f32[2,256]{1,0:T(2,128)S(1)} %pad_maximum_fusion), channel_id=1, replica_groups=mesh['row'=32,'col'=16] {'row'}, dimensions={1}, use_global_device_ids=true | all-gather | bytes 67584 | tf_op jit(solution)/shard_map/all_gather | solution.py:66
  77.3 74.6 %all-gather.8.cloned.1.call-done = bf16[8192,256]{1,0:T(8,128)(2,1)} async-done(((bf16[256,256]{1,0:T(8,128)(2,1)}), bf16[8192,256]{1,0:T(8,128)(2,1)}) %all-gather.8.cloned.1.call-update) | async-done | bytes 4194320 | tf_op jit(solution)/shard_map/all_gather | solution.py:65
  151.9 3.3 fusion.112
  155.2 42.2 %while.104 = (s32[]{:T(128)}, f32[32,128]{1,0:T(8,128)S(1)}, s32[6,8]{1,0:T(8,128)S(1)}, pred[6,8]{1,0:T(8,128)(4,1)S(1)}, s32[6,8]{1,0:T(8,128)S(1)}, /*index=5...) while((s32[]{:T(128)}, f32[32,128]{1,0:T(8,128)S(1)}, ...), condition=%wide.region_3.8_spmd, body=%wide.region_0.7_spmd.sunk | while | flops 68558968 | bytes 3252905 | solution.py:29
  197.5 60.4 %pmax.28 = f32[32,128]{1,0:T(8,128)S(1)} all-reduce(f32[32,128]{1,0:T(8,128)S(1)} %get-tuple-element.1538), channel_id=1, replica_groups=mesh['row'=32,'col'=16] {'col'}, use_global_device_ids=true, to_apply=%region_4.9 | all-reduce | flops 4096 | bytes 32768 | tf_op jit(solution)/shard_map/pmax | solution.py:43
  257.9 45.7 %while.105 = (s32[]{:T(128)}, f32[32,128]{1,0:T(8,128)S(1)}, s32[6,8]{1,0:T(8,128)S(1)}, pred[6,8]{1,0:T(8,128)(4,1)S(1)}, s32[6,8]{1,0:T(8,128)S(1)}, /*index=5...) while((s32[]{:T(128)}, f32[32,128]{1,0:T(8,128)S(1)}, ...), condition=%wide.region_8.13_spmd, body=%wide.region_5.12_spmd.sunk | while | flops 68691064 | bytes 3273425 | solution.py:39
  303.6 15.5 %all-gather = f32[512,128]{1,0:T(8,128)S(1)} all-gather(f32[32,128]{1,0:T(8,128)S(1)} %get-tuple-element.1539), channel_id=2, replica_groups=mesh['row'=32,'col'=16] {'col'}, dimensions={0}, use_global_device_ids=true | all-gather | bytes 278528 | tf_op jit(solution)/shard_map/all_gather | solution.py:44
  319.2 42.5 %while.106 = (s32[]{:T(128)}, f32[64,128]{1,0:T(8,128)S(1)}, s32[6,8]{1,0:T(8,128)S(1)}, pred[6,8]{1,0:T(8,128)(4,1)S(1)}, s32[6,8]{1,0:T(8,128)S(1)}, /*index=5...) while((s32[]{:T(128)}, f32[64,128]{1,0:T(8,128)S(1)}, ...), condition=%wide.region_13.18_spmd, body=%wide.region_10.17_spmd.sunk | while | flops 68558968 | bytes 3252905 | solution.py:29
  322.2 2.8 gather_fusion.14
  329.3 2.8 gather_fusion.14
  343.4 2.8 gather_fusion.14
  350.5 2.8 gather_fusion.14
  361.7 105.9 %pmax.29 = bf16[64,128]{1,0:T(8,128)(2,1)S(1)} all-reduce(bf16[64,128]{1,0:T(8,128)(2,1)S(1)} %convert_element_type.12), channel_id=1, replica_groups=mesh['row'=32,'col'=16] {'row'}, use_global_device_ids=true, to_apply=%region_14.19 | all-reduce | flops 8192 | bytes 32768 | tf_op jit(solution)/shard_map/pmax | solution.py:49
  467.6 45.9 %while.107 = (s32[]{:T(128)}, f32[64,128]{1,0:T(8,128)S(1)}, s32[6,8]{1,0:T(8,128)S(1)}, pred[6,8]{1,0:T(8,128)(4,1)S(1)}, s32[6,8]{1,0:T(8,128)S(1)}, /*index=5...) while((s32[]{:T(128)}, f32[64,128]{1,0:T(8,128)S(1)}, ...), condition=%wide.region_18.23_spmd, body=%wide.region_15.22_spmd.sunk | while | flops 68691064 | bytes 3273425 | solution.py:39
  513.5 90.0 %psum.14 = f32[64,128]{1,0:T(8,128)S(1)} all-reduce(f32[64,128]{1,0:T(8,128)S(1)} %get-tuple-element.1541), channel_id=1, replica_groups=mesh['row'=32,'col'=16] {'row'}, use_global_device_ids=true, to_apply=%region_19.24 | all-reduce | flops 8192 | bytes 65536 | tf_op jit(solution)/shard_map/psum | solution.py:52
  603.6 42.2 %while.108 = (s32[]{:T(128)}, f32[32,128]{1,0:T(8,128)S(1)}, s32[6,8]{1,0:T(8,128)S(1)}, pred[6,8]{1,0:T(8,128)(4,1)S(1)}, s32[6,8]{1,0:T(8,128)S(1)}, /*index=5...) while((s32[]{:T(128)}, f32[32,128]{1,0:T(8,128)S(1)}, ...), condition=%wide.region_23.28_spmd, body=%wide.region_20.27_spmd.sunk | while | flops 68558968 | bytes 3252905 | solution.py:29
  645.8 58.2 %pmax.30 = f32[32,128]{1,0:T(8,128)S(1)} all-reduce(f32[32,128]{1,0:T(8,128)S(1)} %get-tuple-element.1542), channel_id=1, replica_groups=mesh['row'=32,'col'=16] {'col'}, use_global_device_ids=true, to_apply=%region_24.29 | all-reduce | flops 4096 | bytes 32768 | tf_op jit(solution)/shard_map/pmax | solution.py:43
  704.0 45.7 %while.109 = (s32[]{:T(128)}, f32[32,128]{1,0:T(8,128)S(1)}, s32[6,8]{1,0:T(8,128)S(1)}, pred[6,8]{1,0:T(8,128)(4,1)S(1)}, s32[6,8]{1,0:T(8,128)S(1)}, /*index=5...) while((s32[]{:T(128)}, f32[32,128]{1,0:T(8,128)S(1)}, ...), condition=%wide.region_28.33_spmd, body=%wide.region_25.32_spmd.sunk | while | flops 68691064 | bytes 3273425 | solution.py:39
  749.7 15.5 %all-gather.1 = f32[512,128]{1,0:T(8,128)S(1)} all-gather(f32[32,128]{1,0:T(8,128)S(1)} %get-tuple-element.1543), channel_id=3, replica_groups=mesh['row'=32,'col'=16] {'col'}, dimensions={0}, use_global_device_ids=true | all-gather | bytes 278528 | tf_op jit(solution)/shard_map/all_gather | solution.py:44
  765.3 42.5 %while.110 = (s32[]{:T(128)}, f32[64,128]{1,0:T(8,128)S(1)}, s32[6,8]{1,0:T(8,128)S(1)}, pred[6,8]{1,0:T(8,128)(4,1)S(1)}, s32[6,8]{1,0:T(8,128)S(1)}, /*index=5...) while((s32[]{:T(128)}, f32[64,128]{1,0:T(8,128)S(1)}, ...), condition=%wide.region_33.38_spmd, body=%wide.region_30.37_spmd.sunk | while | flops 68558968 | bytes 3252905 | solution.py:29
  807.8 109.2 %pmax.31 = bf16[64,128]{1,0:T(8,128)(2,1)S(1)} all-reduce(bf16[64,128]{1,0:T(8,128)(2,1)S(1)} %convert_element_type.14), channel_id=1, replica_groups=mesh['row'=32,'col'=16] {'row'}, use_global_device_ids=true, to_apply=%region_34.39 | all-reduce | flops 8192 | bytes 32768 | tf_op jit(solution)/shard_map/pmax | solution.py:49
  917.0 45.9 %while.111 = (s32[]{:T(128)}, f32[64,128]{1,0:T(8,128)S(1)}, s32[6,8]{1,0:T(8,128)S(1)}, pred[6,8]{1,0:T(8,128)(4,1)S(1)}, s32[6,8]{1,0:T(8,128)S(1)}, /*index=5...) while((s32[]{:T(128)}, f32[64,128]{1,0:T(8,128)S(1)}, ...), condition=%wide.region_38.43_spmd, body=%wide.region_35.42_spmd.sunk | while | flops 68691064 | bytes 3273425 | solution.py:39
  963.0 90.0 %psum.15 = f32[64,128]{1,0:T(8,128)S(1)} all-reduce(f32[64,128]{1,0:T(8,128)S(1)} %get-tuple-element.1545), channel_id=1, replica_groups=mesh['row'=32,'col'=16] {'row'}, use_global_device_ids=true, to_apply=%region_39.44 | all-reduce | flops 8192 | bytes 65536 | tf_op jit(solution)/shard_map/psum | solution.py:52
  (775 shorter events, 347.0 us)
Async XLA Ops:
  7.2 67.8 %all-gather.6.cloned.1.call-start = ((), (), s32[]{:S(2)}) async-start(), calls=%async_computation | async-start | bytes 2228224 | tf_op jit(solution)/shard_map/all_gather | solution.py:63
  7.9 144.0 %all-gather.8.cloned.1.call-start = ((), (), s32[]{:S(2)}) async-start(), calls=%async_computation.1 | async-start | bytes 4325376 | tf_op jit(solution)/shard_map/all_gather | solution.py:65
  75.0 80.3 %copy-start = (bf16[4096,256]{1,0:T(8,128)(2,1)S(1)}, bf16[4096,256]{1,0:T(8,128)(2,1)}, u32[]{:S(2)}) copy-start(bf16[4096,256]{1,0:T(8,128)(2,1)} %all-gather.6.cloned.1.call-done) | copy-start | bytes 6291460
Sparse Core Ops, SparseCore 0:
  11.0 63.9 all-gather.5
  77.1 74.7 all-gather.7
